TPU v7x, 128 devices: a whole 4x4x4 slice. The times are simulated.
128 devices in a mesh: gx: 16 (over x, z_hi, core), gy: 8 (over y, z_lo).
Axes of the slice: x: 4, y: 4, z: 4 (z_hi: 2, z_lo: 2; z = z_hi * 2 + z_lo), core: 2. Of those that a mesh axis runs over, the one named last changes fastest.
Arguments:
- disc_pos: float32 [2, 64, 256, 128], P(None, 'gy', 'gx'), may hold values from 0 to 1
- disc_vel: float32 [2, 64, 256, 128], P(None, 'gy', 'gx'), may hold values from -3 to 3
- radius: float32 [64, 256, 128], P('gy', 'gx'), may hold values from 0.04 to 0.08
- bond_list: int32 [4, 64, 256, 128], P(None, 'gy', 'gx'), may hold values from 0 to 127
- contact_mask: int32 [8, 64, 256], P(None, 'gy', 'gx'), may hold values 0 or 1
- remap_block: int32 [128, 128, 2], P(('gx', 'gy')), may hold values from -1 to 127, as said below
- ocean_state: float32 [4, 48, 256, 2048], P(None, None, 'gy', 'gx'), may hold values from -6 to 6
- mix_coef: float32 [48, 256, 2048], P(None, 'gy', 'gx'), may hold values from 0.02 to 0.2
- remap_cell: int32 [128, 128, 2], P(('gx', 'gy')), may hold values from 0 to 4095
- fold_perm: int32 [2048], P('gx'), may hold values from 0 to 2047, as said below
Outputs:
- pos_next: float32 [2, 64, 256, 128], P(None, 'gy', 'gx')
- vel_next: float32 [2, 64, 256, 128], P(None, 'gy', 'gx')
- ocean_next: float32 [4, 48, 256, 2048], P(None, None, 'gy', 'gx')
Inputs may be any that keep to these rules, and one draw needn't show every extreme that they name: `remap_block`: for each ice tile, every one of its 128 local blocks stands in exactly one slot and the other slots hold -1; in every draw some ocean tile gets all 2 of its slots filled by every ice tile. `fold_perm`: A permutation of the 2048 columns.
All inputs are finite; a program needn't handle non-finite values. No bound on the sum of `contact_mask` on one device may be relied on, other than what follows from the above.
Results may differ from a plain program's by a relative error of at most 0.0003.
Values sent between devices are 32-bit elements; how exact they have to be, the bound alone decides.
A program may use at most 128 MiB of HBM per device.

v0:
```python
import jax
import jax.numpy as jnp
from jax import lax
from jax.sharding import PartitionSpec as P

BONDS = 4
SUB = 3


SOFTEN = 0.0001
STIFFNESS = 2.0
BOND_STIFF = 0.1
TIME_STEP = 0.05
DRAG_ICE = 15.0
DRAG_BACK = 0.5
VERT_MIX = 0.1
SPIN_RATE = 0.3
ALL_SHIFTS = ((-1, -1), (-1, 0), (-1, 1), (0, -1), (0, 0), (0, 1), (1, -1), (1, 0), (1, 1))


def with_halo(block, sides, width, periodic):
    for axis, dim in sides:
        count = lax.axis_size(axis)
        forward = [(i, i + 1) for i in range(count - 1)]
        if periodic:
            forward.append((count - 1, 0))
        backward = [(target, source) for source, target in forward]
        low = lax.ppermute(
            lax.slice_in_dim(block, block.shape[dim] - width, None, axis=dim), axis, forward
        )
        high = lax.ppermute(lax.slice_in_dim(block, 0, width, axis=dim), axis, backward)
        block = jnp.concatenate([low, block, high], axis=dim)
    return block


def pair_force(own, other, shift_y, shift_x):
    sep_x = other[0][..., None, :] + shift_x - own[0][..., :, None]
    sep_y = other[1][..., None, :] + shift_y - own[1][..., :, None]
    distance = jnp.sqrt(sep_x * sep_x + sep_y * sep_y + SOFTEN)
    push = (
        STIFFNESS
        * jnp.maximum(own[2][..., :, None] + other[2][..., None, :] - distance, 0.0)
        / distance
    )
    return jnp.stack([-jnp.sum(push * sep_x, axis=-1), -jnp.sum(push * sep_y, axis=-1)])


def send_slots(values):
    return lax.all_to_all(values, ("gx", "gy"), split_axis=1, concat_axis=1, tiled=True)


def return_slots(values):
    return lax.all_to_all(values, ("gx", "gy"), split_axis=1, concat_axis=1, tiled=True)


def body(
    disc_pos,
    disc_vel,
    radius,
    bond_list,
    contact_mask,
    remap_block,
    ocean_state,
    mix_coef,
    remap_cell,
    fold_perm,
):
    rows_dev, cols_dev, disc_count = radius.shape
    block_count = rows_dev * cols_dev
    lat_tiles = lax.axis_size("gy")
    total_rows = rows_dev * lat_tiles
    global_rows = lax.axis_index("gy") * rows_dev + jnp.arange(rows_dev, dtype=jnp.int32)
    masked = contact_mask.astype(jnp.float32)
    weights = []
    counter = 0
    for shift_y, shift_x in ALL_SHIFTS:
        if shift_y == 0 and shift_x == 0:
            weights.append(jnp.ones((rows_dev, cols_dev), jnp.float32))
        else:
            inside = ((global_rows + shift_y >= 0) & (global_rows + shift_y < total_rows)).astype(
                jnp.float32
            )
            weights.append(masked[counter] * inside[:, None])
            counter = counter + 1
    mass = (radius / 0.06) ** 2
    disc_ids = jnp.arange(disc_count, dtype=jnp.int32)
    counts = jnp.zeros((rows_dev, cols_dev, disc_count, disc_count), jnp.float32)
    for partner in range(BONDS):
        counts = counts + (bond_list[partner][..., None] == disc_ids).astype(jnp.float32)
    position, velocity = (disc_pos, disc_vel)
    for substep in range(SUB):
        state = jnp.concatenate([position, radius[None]], axis=0)
        wide = with_halo(state, (("gx", 2),), 1, True)
        wide = with_halo(wide, (("gy", 1),), 1, False)
        contact = jnp.zeros((2, rows_dev, cols_dev, disc_count), jnp.float32)
        for index, (shift_y, shift_x) in enumerate(ALL_SHIFTS):
            other = wide[
                :, 1 + shift_y : 1 + shift_y + rows_dev, 1 + shift_x : 1 + shift_x + cols_dev
            ]
            contact = (
                contact
                + pair_force(state, other, float(shift_y), float(shift_x))
                * weights[index][None, :, :, None]
            )
        bonded = jnp.einsum("yxij,cyxj->cyxi", counts, position, precision=lax.Precision.HIGHEST)
        force = contact + BOND_STIFF * (bonded - BONDS * position)
        velocity = velocity + force / mass
        position = position + TIME_STEP * velocity
    impulse = (DRAG_ICE * jnp.sum(radius * radius * velocity, axis=-1)).reshape(2, block_count)
    source_count, tile_count, capacity = remap_block.shape
    selector = (
        remap_block[0].reshape(-1)[:, None] == jnp.arange(block_count, dtype=jnp.int32)[None]
    ).astype(jnp.float32)
    outgoing = jnp.dot(impulse, selector.T, precision=lax.Precision.HIGHEST).reshape(
        2, tile_count, capacity
    )
    arrived = send_slots(outgoing)
    layers, tile_rows, tile_cols = mix_coef.shape
    cells = remap_cell[0].reshape(-1)
    forcing = jax.ops.segment_sum(
        arrived.reshape(2, -1).T, cells, num_segments=tile_rows * tile_cols
    ).T
    forcing = forcing.reshape(2, tile_rows, tile_cols)
    lon_wide = with_halo(ocean_state, (("gx", 3),), 1, True)
    lat_wide = with_halo(ocean_state, (("gy", 2),), 1, False)
    top_row = ocean_state[:, :, tile_rows - 1]
    piece = lax.all_gather(top_row, "gx", axis=2, tiled=True)
    width = piece.shape[2]
    column_ids = jnp.arange(width, dtype=jnp.int32)
    picker = (column_ids[:, None] == fold_perm[None, :]).astype(jnp.float32)
    mirrored = jnp.einsum("fkw,wx->fkx", piece, picker, precision=lax.Precision.HIGHEST)
    signs = jnp.array([-1.0, -1.0, 1.0, 1.0], jnp.float32)[:, None, None]
    mirrored = signs * mirrored
    north = lat_wide[:, :, 2:]
    is_top = lax.axis_index("gy") == lat_tiles - 1
    last_row = jnp.where(is_top, mirrored, north[:, :, tile_rows - 1])
    north = jnp.concatenate([north[:, :, : tile_rows - 1], last_row[:, :, None]], axis=2)
    south = lat_wide[:, :, :tile_rows]
    east = lon_wide[..., 2:]
    west = lon_wide[..., :tile_cols]
    laplace = east + west + north + south - 4.0 * ocean_state
    above = jnp.concatenate([ocean_state[:, :1], ocean_state[:, :-1]], axis=1)
    below = jnp.concatenate([ocean_state[:, 1:], ocean_state[:, -1:]], axis=1)
    vertical = above + below - 2.0 * ocean_state
    updated = ocean_state + mix_coef[None] * laplace + VERT_MIX * vertical
    latitude = (lax.axis_index("gy") * tile_rows + jnp.arange(tile_rows, dtype=jnp.int32)).astype(
        jnp.float32
    )
    coriolis = (SPIN_RATE * (2.0 * (latitude + 0.5) / (tile_rows * lat_tiles) - 1.0))[None, :, None]
    updated = updated.at[0].add(coriolis * ocean_state[1])
    updated = updated.at[1].add(-coriolis * ocean_state[0])
    updated = updated.at[0:2, 0].add(forcing)
    surface = updated[0:2, 0].reshape(2, tile_rows * tile_cols)
    picked = jnp.take(surface, cells, axis=1).reshape(2, tile_count, capacity)
    returned = return_slots(picked)
    per_block = jnp.dot(returned.reshape(2, -1), selector, precision=lax.Precision.HIGHEST)
    per_block = per_block.reshape(2, rows_dev, cols_dev)
    vel_next = velocity + DRAG_BACK * (per_block[..., None] - velocity)
    return (position, vel_next, updated)


def solution(mesh):
    in_specs = (
        P(None, "gy", "gx", None),
        P(None, "gy", "gx", None),
        P("gy", "gx", None),
        P(None, "gy", "gx", None),
        P(None, "gy", "gx"),
        P(("gx", "gy"), None, None),
        P(None, None, "gy", "gx"),
        P(None, "gy", "gx"),
        P(("gx", "gy"), None, None),
        P("gx"),
    )
    out_specs = (P(None, "gy", "gx", None), P(None, "gy", "gx", None), P(None, None, "gy", "gx"))
    return jax.shard_map(body, mesh=mesh, in_specs=in_specs, out_specs=out_specs, check_vma=False)
```

profile of v0, /device:TPU:1, one launch (start us, length us, event | category | flops | bytes accessed | tf_op | source)
XLA Modules:
  0.0 550.7 jit_solution(5588566302574882793)
XLA Ops:
  9.4 5.0 collective-permute-start.15
  22.2 6.6 %fusion.379 = (f32[4,48,32,1]{3,2,1,0:T(8,128)}, f32[4,48,32,1]{3,2,1,0:T(8,128)}) fusion(f32[4,48,32,128]{3,2,1,0:T(8,128)} %param.23), kind=kLoop, calls=%fused_computation.612 | loop fusion | bytes 98304 | tf_op jit(solution)/shard_map/slice | solution.py:31
  28.8 3.7 copy.112
  53.6 4.9 collective-permute-start.2
  61.9 56.2 %fusion.3 = (f32[8,16,128]{2,1,0:T(8,128)S(1)}, f32[8,16,128]{2,1,0:T(8,128)S(1)}, f32[8,16,128]{2,1,0:T(8,128)S(1)}, f32[8,16,128]{2,1,0:T(8,128)S(1)}, f32[8,1...) fusion(f32[8,16,128]{2,1,0:T(8,128)S(1)} %copy-done.10, ...), kind=kLoop, calls=%fused_computation.116 | loop fusion | flops 188547072 | bytes 1966080 | tf_op jit(solution)/shard_map/reduce_sum | solution.py:45
  118.2 37.8 %fusion.12 = (f32[8,16,128]{2,1,0:T(8,128)S(1)}, f32[8,16,128]{2,1,0:T(8,128)S(1)}, f32[8,16,128]{2,1,0:T(8,128)S(1)}, f32[8,16,128]{2,1,0:T(8,128)S(1)}, f32[8,...) fusion(f32[8,16,128]{2,1,0:T(8,128)S(1)} %bitcast.298, f32[8,16,128]{2,1,0:T(8,128)S(1)} %copy-done.10, ...), kind=kLoop, calls=%fused_computation.125 | loop fusion | flops 94273536 | bytes 1179648 | tf_op jit(solution)/shard_map/reduce_sum | solution.py:45
  156.4 33.2 %multiply_add_fusion.3 = (f32[2,8,16,128]{3,0,2,1:T(2,128)S(1)}, f32[2,8,16,128]{3,0,2,1:T(2,128)S(1)}) fusion(f32[2,8,16,128]{3,2,1,0:T(8,128)S(1)} %copy-done.2, f32[8,16,128]{2,1,0:T(8,128)S(1)} %copy-done.7, s32[8,16,128]{2,1,0:T(8,128)S(1)} %copy-done.13, s32[8,16,128]{2,1,0:T(8,128)S(1)} %copy-done.14, s32[8,16,128]{2,1,0:T(8,128)S(1)} %copy-done.12, ...), kind=kOutput, calls=%fused_computation.519 | convolution fusion | flops 74481664 | bytes 2035712 | tf_op jit(solution)/shard_map/yxij,cyxj->cyxi/dot_general | solution.py:105
  189.7 4.0 collective-permute-start.4
  194.5 4.1 collective-permute-done.5
  200.1 4.6 collective-permute-start.6
  207.0 56.2 %fusion.83 = (f32[8,16,128]{2,1,0:T(8,128)S(1)}, f32[8,16,128]{2,1,0:T(8,128)S(1)}, f32[8,16,128]{2,1,0:T(8,128)S(1)}, f32[8,16,128]{2,1,0:T(8,128)S(1)}, f32[8,...) fusion(f32[8,16,128]{2,1,0:T(8,128)S(1)} %bitcast.402, ...), kind=kLoop, calls=%fused_computation.196 | loop fusion | flops 188547072 | bytes 1966080 | tf_op jit(solution)/shard_map/reduce_sum | solution.py:45
  263.2 37.8 %fusion.92 = (f32[8,16,128]{2,1,0:T(8,128)S(1)}, f32[8,16,128]{2,1,0:T(8,128)S(1)}, f32[8,16,128]{2,1,0:T(8,128)S(1)}, f32[8,16,128]{2,1,0:T(8,128)S(1)}, f32[8,...) fusion(f32[8,16,128]{2,1,0:T(8,128)S(1)} %bitcast.292, f32[8,16,128]{2,1,0:T(8,128)S(1)} %bitcast.403, ...), kind=kLoop, calls=%fused_computation.205 | loop fusion | flops 94273536 | bytes 1179648 | tf_op jit(solution)/shard_map/reduce_sum | solution.py:45
  301.3 26.2 %multiply_add_fusion.2 = (f32[2,8,16,128]{3,0,2,1:T(2,128)S(1)}, f32[2,8,16,128]{3,0,2,1:T(2,128)S(1)}) fusion(f32[2,8,16,128]{3,0,2,1:T(2,128)S(1)} %get-tuple-element.275, f32[2,8,16,128]{3,0,2,1:T(2,128)S(1)} %get-tuple-element.276, f32[8,16,128]{2,1,0:T(8,128)S(1)} %copy-done.7, s32[8,16,128]{2,1,0:T(8,128)S(1)} %copy-done.13, ...), kind=kOutput, calls=%fused_computation.518 | convolution fusion | flops 74481664 | bytes 2035712 | tf_op jit(solution)/shard_map/yxij,cyxj->cyxi/dot_general | solution.py:105
  334.4 4.9 collective-permute-start.10
  339.8 3.6 collective-permute-start.12
  344.3 56.2 %fusion.163 = (f32[8,16,128]{2,1,0:T(8,128)S(1)}, f32[8,16,128]{2,1,0:T(8,128)S(1)}, f32[8,16,128]{2,1,0:T(8,128)S(1)}, f32[8,16,128]{2,1,0:T(8,128)S(1)}, f32[8...) fusion(f32[8,16,128]{2,1,0:T(8,128)S(1)} %bitcast.398, ...), kind=kLoop, calls=%fused_computation.276 | loop fusion | flops 188547072 | bytes 1966080 | tf_op jit(solution)/shard_map/reduce_sum | solution.py:45
  400.5 37.8 %fusion.172 = (f32[8,16,128]{2,1,0:T(8,128)S(1)}, f32[8,16,128]{2,1,0:T(8,128)S(1)}, f32[8,16,128]{2,1,0:T(8,128)S(1)}, f32[8,16,128]{2,1,0:T(8,128)S(1)}, f32[8...) fusion(f32[8,16,128]{2,1,0:T(8,128)S(1)} %bitcast.304, f32[8,16,128]{2,1,0:T(8,128)S(1)} %bitcast.399, ...), kind=kLoop, calls=%fused_computation.285 | loop fusion | flops 94273536 | bytes 1179648 | tf_op jit(solution)/shard_map/reduce_sum | solution.py:45
  438.6 29.0 %multiply_reduce_fusion = (f32[2,8,16]{0,2,1:T(8,128)S(1)}, f32[2,8,16,128]{3,0,2,1:T(2,128)}) fusion(f32[8,16,128]{2,1,0:T(8,128)S(1)} %copy-done.8, f32[2,8,16,128]{3,0,2,1:T(2,128)S(1)} %get-tuple-element.278, f32[8,16,128]{2,1,0:T(8,128)S(1)} %copy-done.7, f32[2,8,16,128]{3,0,2,1:T(2,128)S(1)} %get-tuple-element.277, s32[8,16,128]{2,1,0:T(8,128)S(1)} %copy-done.13, ...), kind=kOutput, calls=%fused_computation.516 | convolution fusion | flops 74481408 | bytes 1971200 | tf_op jit(solution)/shard_map/yxij,cyxj->cyxi/dot_general | solution.py:105
  468.7 13.7 %all-to-all-start = ((f32[2,128,2]{0,2,1:T(2,128)}), f32[2,128,2]{0,2,1:T(2,128)S(1)}, u32[]{:S(2)}, u32[]{:S(2)}) async-start(f32[2,128,2]{0,2,1:T(2,128)} %copy.95), calls=%async_computation | async-start | bytes 262144 | tf_op jit(solution)/shard_map/all_to_all | solution.py:49
  485.9 4.4 copy.86
  490.2 4.4 copy.88
  503.8 9.0 %fusion.259 = f32[4,48,32,128]{3,2,1,0:T(8,128)} fusion(f32[4,48,32,128]{3,2,1,0:T(8,128)S(1)} %copy-done, f32[4,48,1,128]{3,2,1,0:T(1,128)} %bitcast.155, f32[4,48,32,1]{3,2,1,0:T(8,128)} %copy.88, f32[4,48,32,1]{3,2,1,0:T(8,128)} %copy.86, f32[4,48,1,128]{3,2,1,0:T(1,128)S(1)} %bitcast.277, f32[4,48,31,128]{3,2,1,0:T(8,128)} %slice.724, ...), kind=kLoop, calls=%fused_computation.378 | loop fusion | flops 14155776 | bytes 16662528 | tf_op jit(solution)/shard_map/add | solution.py:145
  521.8 9.8 %all-to-all-start.1 = ((f32[2,128,2]{2,0,1:T(2,128)}), f32[2,128,2]{2,0,1:T(2,128)S(1)}, u32[]{:S(2)}, u32[]{:S(2)}) async-start(f32[2,128,2]{2,0,1:T(2,128)} %broadcast_select_fusion), calls=%async_computation.1 | async-start | bytes 262144 | tf_op jit(solution)/shard_map/all_to_all | solution.py:53
  531.8 9.8 %all-to-all-done.1 = f32[2,128,2]{2,0,1:T(2,128)S(1)} async-done(((f32[2,128,2]{2,0,1:T(2,128)}), f32[2,128,2]{2,0,1:T(2,128)S(1)}, u32[]{:S(2)}, u32[]{:S(2)}) %all-to-all-start.1) | async-done | bytes 2080 | tf_op jit(solution)/shard_map/all_to_all | solution.py:53
  (216 shorter events, 72.6 us)
Async XLA Ops:
  7.2 494.2 %all-gather.3.cloned.1.call-start = ((), (), s32[]{:S(2)}) async-start(), calls=%async_computation.2 | async-start | bytes 1671168 | tf_op jit(solution)/shard_map/all_gather | solution.py:127
  9.4 494.3 %collective-permute-start.15 = (f32[4,48,1,128]{3,1,0,2:T(8,128)}, f32[4,48,1,128]{3,1,0,2:T(8,128)}, u32[]{:S(2)}, u32[]{:S(2)}) collective-permute-start(f32[4,48,1,128]{3,1,0,2:T(8,128)} %bitcast.279), channel_id=1, source_target_pairs={{0,1},{1,2},{2,3},{3,4},{4,5},{5,6},{6,7},{8,9},{9,10},{10,11},{11... | collective-permute-start | bytes 294920 | tf_op jit(solution)/shard_map/ppermute | solution.py:28
  16.8 34.6 %collective-permute-start.1 = (f32[3,8,1,128]{3,0,2,1:T(4,128)}, f32[3,8,1,128]{3,0,2,1:T(4,128)S(1)}, u32[]{:S(2)}, u32[]{:S(2)}) collective-permute-start(f32[3,8,1,128]{3,0,2,1:T(4,128)} %get-tuple-element.143), channel_id=1, source_target_pairs={{8,0},{16,8},{24,16},{32,24},{40,32},{48,40},{56,48},{64,56},{72,6... | collective-permute-start | bytes 36872 | tf_op jit(solution)/shard_map/ppermute | solution.py:31
  17.7 33.7 %collective-permute-start = (f32[3,8,1,128]{3,0,2,1:T(4,128)}, f32[3,8,1,128]{3,0,2,1:T(4,128)}, u32[]{:S(2)}, u32[]{:S(2)}) collective-permute-start(f32[3,8,1,128]{3,0,2,1:T(4,128)} %get-tuple-element.261), channel_id=1, source_target_pairs={{0,8},{8,16},{16,24},{24,32},{32,40},{40,48},{48,56},{56,64},{64,7... | collective-permute-start | bytes 36872 | tf_op jit(solution)/shard_map/ppermute | solution.py:28
  20.9 480.4 %collective-permute-start.14 = (f32[4,48,1,128]{3,1,0,2:T(8,128)}, f32[4,48,1,128]{3,1,0,2:T(8,128)}, u32[]{:S(2)}, u32[]{:S(2)}) collective-permute-start(f32[4,48,1,128]{3,1,0,2:T(8,128)} %bitcast.173), channel_id=1, source_target_pairs={{1,0},{2,1},{3,2},{4,3},{5,4},{6,5},{7,6},{9,8},{10,9},{11,10},{12... | collective-permute-start | bytes 294920 | tf_op jit(solution)/shard_map/ppermute | solution.py:31
  32.6 457.7 %collective-permute-start.13 = (f32[4,48,32,1]{1,2,3,0:T(8,128)}, f32[4,48,32,1]{1,2,3,0:T(8,128)}, u32[]{:S(2)}, u32[]{:S(2)}) collective-permute-start(f32[4,48,32,1]{1,2,3,0:T(8,128)} %copy.112), channel_id=1, source_target_pairs={{0,8},{8,16},{16,24},{24,32},{32,40},{40,48},{48,56},{56,64},{64,7... | collective-permute-start | bytes 73736 | tf_op jit(solution)/shard_map/ppermute | solution.py:28
  52.3 7.3 %collective-permute-start.3 = (f32[3,1,18,128]{3,0,2,1:T(4,128)S(1)}, f32[3,1,18,128]{3,0,2,1:T(4,128)S(1)}, u32[]{:S(2)}, u32[]{:S(2)}) collective-permute-start(f32[3,1,18,128]{3,0,2,1:T(4,128)S(1)} %get-tuple-element.211), channel_id=1, source_target_pairs={{1,0},{2,1},{3,2},{4,3},{5,4},{6,5},{7,6},{9,8},{10,9},{11,10},{12... | collective-permute-start | bytes 82952 | tf_op jit(solution)/shard_map/ppermute | solution.py:31
  53.6 6.0 %collective-permute-start.2 = (f32[3,1,18,128]{3,0,2,1:T(4,128)S(1)}, f32[3,1,18,128]{3,0,2,1:T(4,128)S(1)}, u32[]{:S(2)}, u32[]{:S(2)}) collective-permute-start(f32[3,1,18,128]{3,0,2,1:T(4,128)S(1)} %get-tuple-element.212), channel_id=1, source_target_pairs={{0,1},{1,2},{2,3},{3,4},{4,5},{5,6},{6,7},{8,9},{9,10},{10,11},{11... | collective-permute-start | bytes 82952 | tf_op jit(solution)/shard_map/ppermute | solution.py:28
  118.1 38.2 %copy-start.7 = (f32[8,16,128]{2,1,0:T(8,128)S(1)}, f32[8,16,128]{2,1,0:T(8,128)}, u32[]{:S(2)}) copy-start(f32[8,16,128]{2,1,0:T(8,128)} %get-tuple-element.257) | copy-start | bytes 196612
  118.1 38.2 %copy-start.11 = (s32[8,16,128]{2,1,0:T(8,128)S(1)}, s32[8,16,128]{2,1,0:T(8,128)}, u32[]{:S(2)}) copy-start(s32[8,16,128]{2,1,0:T(8,128)} %get-tuple-element.231) | copy-start | bytes 196612
  118.1 38.2 %copy-start.12 = (s32[8,16,128]{2,1,0:T(8,128)S(1)}, s32[8,16,128]{2,1,0:T(8,128)}, u32[]{:S(2)}) copy-start(s32[8,16,128]{2,1,0:T(8,128)} %get-tuple-element.232) | copy-start | bytes 196612
  118.1 38.2 %copy-start.13 = (s32[8,16,128]{2,1,0:T(8,128)S(1)}, s32[8,16,128]{2,1,0:T(8,128)}, u32[]{:S(2)}) copy-start(s32[8,16,128]{2,1,0:T(8,128)} %get-tuple-element.233) | copy-start | bytes 196612
  118.1 38.2 %copy-start.14 = (s32[8,16,128]{2,1,0:T(8,128)S(1)}, s32[8,16,128]{2,1,0:T(8,128)}, u32[]{:S(2)}) copy-start(s32[8,16,128]{2,1,0:T(8,128)} %get-tuple-element.234) | copy-start | bytes 196612
  189.7 4.9 collective-permute-start.4
  193.7 5.0 collective-permute-start.5
  198.8 6.4 %collective-permute-start.7 = (f32[3,1,18,128]{3,0,2,1:T(4,128)S(1)}, f32[3,1,18,128]{3,0,2,1:T(4,128)S(1)}, u32[]{:S(2)}, u32[]{:S(2)}) collective-permute-start(f32[3,1,18,128]{3,0,2,1:T(4,128)S(1)} %get-tuple-element.209), channel_id=1, source_target_pairs={{1,0},{2,1},{3,2},{4,3},{5,4},{6,5},{7,6},{9,8},{10,9},{11,10},{12... | collective-permute-start | bytes 82952 | tf_op jit(solution)/shard_map/ppermute | solution.py:31
  200.1 6.0 %collective-permute-start.6 = (f32[3,1,18,128]{3,0,2,1:T(4,128)S(1)}, f32[3,1,18,128]{3,0,2,1:T(4,128)S(1)}, u32[]{:S(2)}, u32[]{:S(2)}) collective-permute-start(f32[3,1,18,128]{3,0,2,1:T(4,128)S(1)} %get-tuple-element.210), channel_id=1, source_target_pairs={{0,1},{1,2},{2,3},{3,4},{4,5},{5,6},{6,7},{8,9},{9,10},{10,11},{11... | collective-permute-start | bytes 82952 | tf_op jit(solution)/shard_map/ppermute | solution.py:28
  327.5 1.9 collective-permute-start.8
  328.3 4.7 collective-permute-start.9
  333.1 6.6 %collective-permute-start.11 = (f32[3,1,18,128]{3,0,2,1:T(4,128)S(1)}, f32[3,1,18,128]{3,0,2,1:T(4,128)S(1)}, u32[]{:S(2)}, u32[]{:S(2)}) collective-permute-start(f32[3,1,18,128]{3,0,2,1:T(4,128)S(1)} %get-tuple-element.207), channel_id=1, source_target_pairs={{1,0},{2,1},{3,2},{4,3},{5,4},{6,5},{7,6},{9,8},{10,9},{11,10},{12... | collective-permute-start | bytes 82952 | tf_op jit(solution)/shard_map/ppermute | solution.py:31
  334.4 9.0 %collective-permute-start.10 = (f32[3,1,18,128]{3,0,2,1:T(4,128)S(1)}, f32[3,1,18,128]{3,0,2,1:T(4,128)S(1)}, u32[]{:S(2)}, u32[]{:S(2)}) collective-permute-start(f32[3,1,18,128]{3,0,2,1:T(4,128)S(1)} %get-tuple-element.208), channel_id=1, source_target_pairs={{0,1},{1,2},{2,3},{3,4},{4,5},{5,6},{6,7},{8,9},{9,10},{10,11},{11... | collective-permute-start | bytes 82952 | tf_op jit(solution)/shard_map/ppermute | solution.py:28
  339.8 146.1 %collective-permute-start.12 = (f32[4,48,32,1]{1,2,3,0:T(8,128)}, f32[4,48,32,1]{1,2,3,0:T(8,128)}, u32[]{:S(2)}, u32[]{:S(2)}) collective-permute-start(f32[4,48,32,1]{1,2,3,0:T(8,128)} %copy.111), channel_id=1, source_target_pairs={{8,0},{16,8},{24,16},{32,24},{40,32},{48,40},{56,48},{64,56},{72,6... | collective-permute-start | bytes 73736 | tf_op jit(solution)/shard_map/ppermute | solution.py:31
  468.7 26.0 %all-to-all-start = ((f32[2,128,2]{0,2,1:T(2,128)}), f32[2,128,2]{0,2,1:T(2,128)S(1)}, u32[]{:S(2)}, u32[]{:S(2)}) async-start(f32[2,128,2]{0,2,1:T(2,128)} %copy.95), calls=%async_computation | async-start | bytes 262144 | tf_op jit(solution)/shard_map/all_to_all | solution.py:49
  521.8 19.8 %all-to-all-start.1 = ((f32[2,128,2]{2,0,1:T(2,128)}), f32[2,128,2]{2,0,1:T(2,128)S(1)}, u32[]{:S(2)}, u32[]{:S(2)}) async-start(f32[2,128,2]{2,0,1:T(2,128)} %broadcast_select_fusion), calls=%async_computation.1 | async-start | bytes 262144 | tf_op jit(solution)/shard_map/all_to_all | solution.py:53
  (25 other events, 580.4 us)
Sparse Core Ops, SparseCore 0:
  10.2 51.0 all-gather.2
where the time goes:
time: 556 us; the launch traced here: 551 us
  other arithmetic  317 us (57%)
  matrix products  91.3 us (16%)
  starting transfers between devices  61.5 us (11%)
  local copies, waits for them, and re-layouts  45.8 us (8%)
  waiting for transfers between devices  19.7 us (4%)
  between operations  15.5 us (3%)
    reduce_sum x6, other arithmetic, pair_force(): jnp.sum(push * sep_x, axis=-1)  282 us
    dot_general x3, matrix products, body(): jnp.einsum('yxij,cyxj->cyxi', counts, position, precision=lax.Precision.H...  88.4 us
    ppermute x8, starting transfers between devices, with_halo(): lax.ppermute(lax.slice_in_dim(block, block.shape[dim] - width, None, axis...  27.7 us
    all_to_all x1, starting transfers between devices, send_slots(): lax.all_to_all(values, ('gx', 'gy'), split_axis=1, concat_axis=1, tiled=T...  13.7 us
  transfers between devices with their start and end apart: 19, of which 6 were waited for; matrix products, arithmetic and copies ran while one was open for 78% of the time, Pallas kernels for 0%

commit v1 on v0

--- a/solution.py
+++ b/solution.py
@@ -1,6 +1,8 @@
 import jax
 import jax.numpy as jnp
 from jax import lax
+from jax.experimental import pallas as pl
+from jax.experimental.pallas import tpu as pltpu
 from jax.sharding import PartitionSpec as P
 
 BONDS = 4
@@ -15,7 +17,6 @@
 DRAG_BACK = 0.5
 VERT_MIX = 0.1
 SPIN_RATE = 0.3
-ALL_SHIFTS = ((-1, -1), (-1, 0), (-1, 1), (0, -1), (0, 0), (0, 1), (1, -1), (1, 0), (1, 1))
 
 
 def with_halo(block, sides, width, periodic):
@@ -33,16 +34,180 @@
     return block
 
 
-def pair_force(own, other, shift_y, shift_x):
-    sep_x = other[0][..., None, :] + shift_x - own[0][..., :, None]
-    sep_y = other[1][..., None, :] + shift_y - own[1][..., :, None]
-    distance = jnp.sqrt(sep_x * sep_x + sep_y * sep_y + SOFTEN)
-    push = (
-        STIFFNESS
-        * jnp.maximum(own[2][..., :, None] + other[2][..., None, :] - distance, 0.0)
-        / distance
-    )
-    return jnp.stack([-jnp.sum(push * sep_x, axis=-1), -jnp.sum(push * sep_y, axis=-1)])
+NEIGHBOURS = ((-1, -1), (-1, 0), (-1, 1), (0, -1), (0, 1), (1, -1), (1, 0), (1, 1))
+
+
+def lane_take(rows, index):
+    return jnp.take_along_axis(rows, index, axis=1, mode="promise_in_bounds")
+
+
+def pair_terms(acc_x, acc_y, own_x, own_y, own_r, other_x, other_y, other_r):
+    sep_x = other_x - own_x
+    sep_y = other_y - own_y
+    inverse = lax.rsqrt(sep_x * sep_x + sep_y * sep_y + SOFTEN)
+    push = jnp.maximum((other_r + own_r) * inverse - 1.0, 0.0)
+    return acc_x + push * sep_x, acc_y + push * sep_y
+
+
+def contact_kernel(
+    wide, pos, vel, rad, bonds, mask, pos_out, vel_out, columns, found, found_t, force, tally, counts, sem
+):
+    rows_dev, cols_dev = wide.shape[1] - 2, pos.shape[1] // (wide.shape[1] - 2)
+    blocks, discs = rad.shape
+    lane = lax.broadcasted_iota(jnp.int32, (8, discs), 1)
+    lane_f = lane.astype(jnp.float32)
+    tri_row = lax.broadcasted_iota(jnp.int32, (discs, 2 * discs), 0)
+    tri_col = lax.broadcasted_iota(jnp.int32, (discs, 2 * discs), 1)
+    triangle = (tri_row <= tri_col).astype(jnp.bfloat16)
+    for comp in range(2):
+        columns[comp] = pos[comp].T
+    columns[2] = rad[...].T
+
+    def collect(start):
+        def one_row(y, carry):
+            for half in range(cols_dev // 8):
+                x0 = half * 8
+                at = pl.multiple_of(y * cols_dev + x0, 8)
+                own = [pos[0, pl.ds(at, 8), :], pos[1, pl.ds(at, 8), :], rad[pl.ds(at, 8), :]]
+                reach = jnp.max(own[2], axis=1, keepdims=True)
+                low = [jnp.min(own[c], axis=1, keepdims=True) - reach for c in range(2)]
+                high = [jnp.max(own[c], axis=1, keepdims=True) + reach for c in range(2)]
+                weights = mask[pl.ds(at, 8), :]
+                near = []
+                for k, (sy, sx) in enumerate(NEIGHBOURS):
+                    where = (y + 1 + sy, pl.ds(x0 + 1 + sx, 8), slice(None))
+                    nx = wide[(0,) + where] + float(sx)
+                    ny = wide[(1,) + where] + float(sy)
+                    nr = wide[(2,) + where]
+                    close = (nx - nr < high[0]) & (nx + nr > low[0])
+                    close = close & (ny - nr < high[1]) & (ny + nr > low[1])
+                    close = close & (weights[:, k : k + 1] > 0.5)
+                    near.append((nx, ny, nr, close))
+                flags = jnp.concatenate([n[3].astype(jnp.float32) for n in near], axis=0)
+                ranks = jnp.dot(
+                    flags.astype(jnp.bfloat16), triangle, preferred_element_type=jnp.float32
+                )
+                base = jnp.zeros((8, discs), jnp.float32) - start
+                gx = jnp.zeros((8, discs), jnp.float32)
+                gy = jnp.zeros((8, discs), jnp.float32)
+                gr = jnp.full((8, discs), -1.0, jnp.float32)
+                for k in range(8):
+                    nx, ny, nr, _ = near[k]
+                    rank = ranks[8 * k : 8 * k + 8, :discs]
+                    total = ranks[8 * k : 8 * k + 8, discs:]
+                    want = lane_f - base
+                    source = jnp.zeros((8, discs), jnp.int32)
+                    step = discs // 2
+                    while step >= 1:
+                        probe = lane_take(rank, source + (step - 1))
+                        source = jnp.where(probe <= want, source + step, source)
+                        step //= 2
+                    valid = (want >= 0.0) & (want < total)
+                    gx = jnp.where(valid, lane_take(nx, source), gx)
+                    gy = jnp.where(valid, lane_take(ny, source), gy)
+                    gr = jnp.where(valid, lane_take(nr, source), gr)
+                    base = base + total
+                found[0, pl.ds(at, 8), :] = gx
+                found[1, pl.ds(at, 8), :] = gy
+                found[2, pl.ds(at, 8), :] = gr
+                found[3, pl.ds(at, 8), :] = base
+            return carry
+
+        lax.fori_loop(0, rows_dev, one_row, 0)
+        for comp in range(3):
+            found_t[comp] = found[comp].T
+        left = found[3].T[0:8]
+        groups = jnp.clip(jnp.ceil(left * (1.0 / 32.0)), 0.0, 4.0).astype(jnp.int32)
+        passes = jnp.ceil(jnp.max(left, axis=1, keepdims=True) * (1.0 / discs)).astype(jnp.int32)
+        tally[0:8] = groups
+        tally[8:16] = jnp.broadcast_to(passes, (8, discs))
+        copy = pltpu.make_async_copy(tally, counts, sem)
+        copy.start()
+        copy.wait()
+
+    def own_rows(b):
+        return pos[0, pl.ds(b, 1), :], pos[1, pl.ds(b, 1), :], rad[pl.ds(b, 1), :]
+
+    def ghosts(b, own, index, acc):
+        def group(g, acc):
+            for c in range(4):
+                at = pl.ds(pl.multiple_of(g * 32 + c * 8, 8), 8)
+                acc = pair_terms(*acc, *own, *[lane_take(found_t[k, at, :], index) for k in range(3)])
+            return acc
+
+        return lax.fori_loop(0, counts[0, b], group, acc)
+
+    zero = jnp.zeros((8, discs), jnp.float32)
+    collect(0.0)
+
+    def target(b, carry):
+        own = own_rows(b)
+        index = jnp.full((8, discs), b, jnp.int32)
+        acc = (zero, zero)
+        for c in range(discs // 8):
+            at = pl.ds(c * 8, 8)
+            acc = pair_terms(*acc, *own, *[lane_take(columns[k, at, :], index) for k in range(3)])
+        acc = ghosts(b, own, index, acc)
+        for k in range(2):
+            force[k, pl.ds(b, 1), :] = jnp.sum(acc[k], axis=0, keepdims=True)
+        return carry
+
+    lax.fori_loop(0, blocks, target, 0)
+
+    def more(p, carry):
+        collect(p.astype(jnp.float32) * discs)
+
+        def again(b, carry):
+            own = own_rows(b)
+            index = jnp.full((8, discs), b, jnp.int32)
+            acc = ghosts(b, own, index, (zero, zero))
+            for k in range(2):
+                force[k, pl.ds(b, 1), :] += jnp.sum(acc[k], axis=0, keepdims=True)
+            return carry
+
+        return lax.fori_loop(0, blocks, again, carry)
+
+    lax.fori_loop(1, counts[8, 0], more, 0)
+
+    def update(g, carry):
+        at = pl.ds(pl.multiple_of(g * 8, 8), 8)
+        scale = 0.06 / rad[at, :]
+        scale = scale * scale
+        for k in range(2):
+            here = pos[k, at, :]
+            bonded = lane_take(here, bonds[0, at, :])
+            for p in range(1, 4):
+                bonded = bonded + lane_take(here, bonds[p, at, :])
+            total = 0.1 * (bonded - 4.0 * here) - 2.0 * force[k, at, :]
+            speed = vel[k, at, :] + total * scale
+            vel_out[k, at, :] = speed
+            pos_out[k, at, :] = here + 0.05 * speed
+        return carry
+
+    lax.fori_loop(0, blocks // 8, update, 0)
+
+
+def contact_step(wide, pos, vel, rad, bonds, mask):
+    blocks, discs = rad.shape
+    square = jax.ShapeDtypeStruct((2, blocks, discs), jnp.float32)
+    vmem = pl.BlockSpec(memory_space=pltpu.VMEM)
+    return pl.pallas_call(
+        contact_kernel,
+        out_shape=(square, square),
+        in_specs=[vmem] * 6,
+        out_specs=(vmem, vmem),
+        scratch_shapes=[
+            pltpu.VMEM((3, discs, blocks), jnp.float32),
+            pltpu.VMEM((4, blocks, discs), jnp.float32),
+            pltpu.VMEM((3, discs, blocks), jnp.float32),
+            pltpu.VMEM((2, blocks, discs), jnp.float32),
+            pltpu.VMEM((16, blocks), jnp.int32),
+            pltpu.SMEM((16, blocks), jnp.int32),
+            pltpu.SemaphoreType.DMA,
+        ],
+        compiler_params=pltpu.CompilerParams(vmem_limit_bytes=24 << 20),
+        name="contact",
+    )(wide, pos, vel, rad, bonds, mask)
 
 
 def send_slots(values):
@@ -70,42 +235,26 @@
     lat_tiles = lax.axis_size("gy")
     total_rows = rows_dev * lat_tiles
     global_rows = lax.axis_index("gy") * rows_dev + jnp.arange(rows_dev, dtype=jnp.int32)
-    masked = contact_mask.astype(jnp.float32)
     weights = []
-    counter = 0
-    for shift_y, shift_x in ALL_SHIFTS:
-        if shift_y == 0 and shift_x == 0:
-            weights.append(jnp.ones((rows_dev, cols_dev), jnp.float32))
-        else:
-            inside = ((global_rows + shift_y >= 0) & (global_rows + shift_y < total_rows)).astype(
-                jnp.float32
-            )
-            weights.append(masked[counter] * inside[:, None])
-            counter = counter + 1
-    mass = (radius / 0.06) ** 2
-    disc_ids = jnp.arange(disc_count, dtype=jnp.int32)
-    counts = jnp.zeros((rows_dev, cols_dev, disc_count, disc_count), jnp.float32)
-    for partner in range(BONDS):
-        counts = counts + (bond_list[partner][..., None] == disc_ids).astype(jnp.float32)
+    for index, (shift_y, shift_x) in enumerate(NEIGHBOURS):
+        inside = (global_rows + shift_y >= 0) & (global_rows + shift_y < total_rows)
+        weights.append(jnp.where(inside[:, None], contact_mask[index], 0).astype(jnp.float32))
+    mask = jnp.stack(weights, axis=-1).reshape(block_count, 8)
     position, velocity = (disc_pos, disc_vel)
     for substep in range(SUB):
         state = jnp.concatenate([position, radius[None]], axis=0)
         wide = with_halo(state, (("gx", 2),), 1, True)
         wide = with_halo(wide, (("gy", 1),), 1, False)
-        contact = jnp.zeros((2, rows_dev, cols_dev, disc_count), jnp.float32)
-        for index, (shift_y, shift_x) in enumerate(ALL_SHIFTS):
-            other = wide[
-                :, 1 + shift_y : 1 + shift_y + rows_dev, 1 + shift_x : 1 + shift_x + cols_dev
-            ]
-            contact = (
-                contact
-                + pair_force(state, other, float(shift_y), float(shift_x))
-                * weights[index][None, :, :, None]
-            )
-        bonded = jnp.einsum("yxij,cyxj->cyxi", counts, position, precision=lax.Precision.HIGHEST)
-        force = contact + BOND_STIFF * (bonded - BONDS * position)
-        velocity = velocity + force / mass
-        position = position + TIME_STEP * velocity
+        position, velocity = contact_step(
+            wide,
+            position.reshape(2, block_count, disc_count),
+            velocity.reshape(2, block_count, disc_count),
+            radius.reshape(block_count, disc_count),
+            bond_list.reshape(BONDS, block_count, disc_count),
+            mask,
+        )
+        position = position.reshape(disc_pos.shape)
+        velocity = velocity.reshape(disc_pos.shape)
     impulse = (DRAG_ICE * jnp.sum(radius * radius * velocity, axis=-1)).reshape(2, block_count)
     source_count, tile_count, capacity = remap_block.shape
     selector = (

time: 556 us -> 357 us (0.64); the launches traced: 551 us -> 358 us
  other arithmetic: 317 us -> 24 us
  Pallas kernels: 0 us -> 169 us
  matrix products: 91.3 us -> 3 us
  starting transfers between devices: 61.5 us -> 95 us
  local copies, waits for them, and re-layouts: 45.8 us -> 37.6 us
    reduce_sum x6 -> x1, other arithmetic: 282 us -> 0.11 us  [body(): jnp.sum(radius * radius * velocity, axis=-1)]
    pallas_call x0 -> x3, Pallas kernels: none -> 169 us  [contact_step(): pl.pallas_call(contact_kernel, out_shape=(square, square), in_specs=[vmem...]
    dot_general x3 -> x0, matrix products: 88.4 us -> none  [body(): jnp.einsum('yxij,cyxj->cyxi', counts, position, precision=lax.Precision.H...]
    all_to_all x1, starting transfers between devices: 13.7 us -> 50 us  [send_slots(): lax.all_to_all(values, ('gx', 'gy'), split_axis=1, concat_axis=1, tiled=T...]
    unnamed x67 -> x32, local copies, waits for them, and re-layouts: 10.7 us -> 5.08 us
  transfers between devices with their start and end apart: 19 -> 19, of which waited for: 6 -> 5; matrix products, arithmetic and copies ran while one was open for 78% -> 11% of each run, Pallas kernels for 0% -> 47%
where the time goes in v1:
time: 357 us; the launch traced here: 358 us
  Pallas kernels  169 us (47%)
  starting transfers between devices  95 us (27%)
  local copies, waits for them, and re-layouts  37.6 us (11%)
  other arithmetic  24 us (7%)
  waiting for transfers between devices  14.7 us (4%)
  between operations  14.6 us (4%)
    pallas_call x3, Pallas kernels, contact_step(): pl.pallas_call(contact_kernel, out_shape=(square, square), in_specs=[vmem...  169 us
    all_to_all x1, starting transfers between devices, send_slots(): lax.all_to_all(values, ('gx', 'gy'), split_axis=1, concat_axis=1, tiled=T...  50 us
    ppermute x8, starting transfers between devices, with_halo(): lax.ppermute(lax.slice_in_dim(block, block.shape[dim] - width, None, axis...  22.3 us
    add x1, other arithmetic, body(): updated = ocean_state + mix_coef[None] * laplace + VERT_MIX * vertical  13.2 us
    ppermute x8, starting transfers between devices, with_halo(): lax.ppermute(lax.slice_in_dim(block, 0, width, axis=dim), axis, backward)  13 us
    all_to_all x1, waiting for transfers between devices, return_slots(): lax.all_to_all(values, ('gx', 'gy'), split_axis=1, concat_axis=1, tiled=T...  9.81 us
    all_to_all x1, starting transfers between devices, return_slots(): lax.all_to_all(values, ('gx', 'gy'), split_axis=1, concat_axis=1, tiled=T...  9.76 us
    slice x2, local copies, waits for them, and re-layouts, with_halo(): lax.slice_in_dim(block, 0, width, axis=dim)  7.69 us
  transfers between devices with their start and end apart: 19, of which 5 were waited for; matrix products, arithmetic and copies ran while one was open for 11% of the time, Pallas kernels for 47%

profile of v1, /device:TPU:1, one launch (start us, length us, event | category | flops | bytes accessed | tf_op | source)
XLA Modules:
  0.0 357.7 jit_solution(3060813431606617261)
XLA Ops:
  7.2 2.2 fusion.62
  9.4 5.0 %collective-permute-start.15 = (f32[4,48,1,128]{3,1,0,2:T(8,128)S(1)}, f32[4,48,1,128]{3,1,0,2:T(8,128)}, u32[]{:S(2)}, u32[]{:S(2)}) collective-permute-start(f32[4,48,1,128]{3,1,0,2:T(8,128)S(1)} %bitcast.81), channel_id=1, source_target_pairs={{0,1},{1,2},{2,3},{3,4},{4,5},{5,6},{6,7},{8,9},{9,10},{10,11},{11... | collective-permute-start | bytes 294920 | tf_op jit(solution)/shard_map/ppermute | solution.py:29
  16.3 3.3 collective-permute-start
  19.6 5.5 %fusion.63 = (f32[4,48,32,1]{3,2,1,0:T(8,128)S(1)}, f32[4,48,32,1]{3,2,1,0:T(8,128)}) fusion(f32[4,48,32,128]{3,2,1,0:T(8,128)} %param.23), kind=kLoop, calls=%fused_computation.101 | loop fusion | bytes 98304 | tf_op jit(solution)/shard_map/slice | solution.py:32
  25.1 3.0 copy.94
  31.8 6.2 %fusion.60 = (f32[4,47,32,128]{3,2,1,0:T(8,128)}, f32[4,47,32,128]{3,2,1,0:T(8,128)}) fusion(f32[4,48,32,128]{3,2,1,0:T(8,128)} %param.23), kind=kLoop, calls=%fused_computation.98 | loop fusion | bytes 12320768 | tf_op jit(solution)/shard_map/slice | solution.py:292
  42.1 4.0 %collective-permute-start.2 = (f32[3,1,18,128]{3,2,1,0:T(8,128)S(1)}, f32[3,1,18,128]{3,2,1,0:T(8,128)S(1)}, u32[]{:S(2)}, u32[]{:S(2)}) collective-permute-start(f32[3,1,18,128]{3,2,1,0:T(8,128)S(1)} %get-tuple-element.67), channel_id=1, source_target_pairs={{0,1},{1,2},{2,3},{3,4},{4,5},{5,6},{6,7},{8,9},{9,10},{10,11},{11... | collective-permute-start | bytes 82952 | tf_op jit(solution)/shard_map/ppermute | solution.py:29
  47.7 52.3 %contact.3 = (f32[2,128,128]{2,1,0:T(8,128)S(1)}, f32[2,128,128]{2,1,0:T(8,128)S(1)}) custom-call(f32[3,10,18,128]{3,2,1,0:T(8,128)S(1)} %fusion.27.wide, f32[2,128,128]{2,1,0:T(8,128)S(1)} %bitcast.68, f32[2,128,128]{2,1,0:T(8,128)S(1)} %bitcast.76, f32[128,128]{1,0:T(8,128)S(1)} %bitcast.56, s32[4,128,128]{2,1,0:T(8,128)S(1)} %bitcast.65, ...), custom_call_target="tpu_custom_call" | custom-call | tf_op jit(solution)/shard_map/contact/pallas_call | solution.py:194
  100.0 2.8 collective-permute-start.5
  106.1 4.2 %collective-permute-start.6 = (f32[3,1,18,128]{3,2,1,0:T(8,128)S(1)}, f32[3,1,18,128]{3,2,1,0:T(8,128)S(1)}, u32[]{:S(2)}, u32[]{:S(2)}) collective-permute-start(f32[3,1,18,128]{3,2,1,0:T(8,128)S(1)} %get-tuple-element.65), channel_id=1, source_target_pairs={{0,1},{1,2},{2,3},{3,4},{4,5},{5,6},{6,7},{8,9},{9,10},{10,11},{11... | collective-permute-start | bytes 82952 | tf_op jit(solution)/shard_map/ppermute | solution.py:29
  111.4 53.0 %contact.4 = (f32[2,128,128]{2,1,0:T(8,128)S(1)}, f32[2,128,128]{2,1,0:T(8,128)S(1)}) custom-call(f32[3,10,18,128]{3,2,1,0:T(8,128)S(1)} %fusion.31.wide, f32[2,128,128]{2,1,0:T(8,128)S(1)} %get-tuple-element.45.pos, f32[2,128,128]{2,1,0:T(8,128)S(1)} %get-tuple-element.46.vel, f32[128,128]{1,0:T(8,128)S(1)} %bitcast.60, s32[4,128,128]{2,1,0:T(8,128)S(1)} %bitcast.66, ...), custom_call_target="tpu_custom_call" | custom-call | tf_op jit(solution)/shard_map/contact/pallas_call | solution.py:194
  164.4 2.4 collective-permute-start.9
  170.5 4.0 %collective-permute-start.10 = (f32[3,1,18,128]{3,2,1,0:T(8,128)S(1)}, f32[3,1,18,128]{3,2,1,0:T(8,128)S(1)}, u32[]{:S(2)}, u32[]{:S(2)}) collective-permute-start(f32[3,1,18,128]{3,2,1,0:T(8,128)S(1)} %get-tuple-element.63), channel_id=1, source_target_pairs={{0,1},{1,2},{2,3},{3,4},{4,5},{5,6},{6,7},{8,9},{9,10},{10,11},{11... | collective-permute-start | bytes 82952 | tf_op jit(solution)/shard_map/ppermute | solution.py:29
  176.1 63.5 %contact.5 = (f32[2,128,128]{2,1,0:T(8,128)}, f32[2,128,128]{2,1,0:T(8,128)S(1)}) custom-call(f32[3,10,18,128]{3,2,1,0:T(8,128)S(1)} %fusion.35.wide, f32[2,128,128]{2,1,0:T(8,128)S(1)} %get-tuple-element.47.pos, f32[2,128,128]{2,1,0:T(8,128)S(1)} %get-tuple-element.48.vel, f32[128,128]{1,0:T(8,128)S(1)} %bitcast.64, s32[4,128,128]{2,1,0:T(8,128)S(1)} %bitcast.67, ...), custom_call_target="tpu_custom_call" | custom-call | tf_op jit(solution)/shard_map/contact/pallas_call | solution.py:194
  240.8 50.0 %all-to-all-start = ((f32[2,128,2]{0,2,1:T(2,128)}), f32[2,128,2]{0,2,1:T(2,128)S(1)}, u32[]{:S(2)}, u32[]{:S(2)}) async-start(f32[2,128,2]{0,2,1:T(2,128)} %copy.82), calls=%async_computation | async-start | bytes 262144 | tf_op jit(solution)/shard_map/all_to_all | solution.py:214
  290.8 4.0 %slice.222 = f32[4,48,31,128]{3,2,1,0:T(8,128)} slice(f32[4,48,32,128]{3,2,1,0:T(8,128)} %param.23), slice={[0:4], [0:48], [1:32], [0:128]} | slice | bytes 6094848 | tf_op jit(solution)/shard_map/slice | solution.py:286
  295.0 3.6 %copy.76 = f32[4,48,32,1]{3,2,1,0:T(8,128)} copy(f32[4,48,32,1]{1,2,3,0:T(8,128)S(1)} %collective-permute-done.13) | data formatting | bytes 49152 | tf_op jit(solution)/shard_map/ppermute | solution.py:29
  298.7 3.6 %copy.74 = f32[4,48,32,1]{3,2,1,0:T(8,128)} copy(f32[4,48,32,1]{1,2,3,0:T(8,128)S(1)} %collective-permute-done.12) | data formatting | bytes 49152 | tf_op jit(solution)/shard_map/ppermute | solution.py:32
  305.1 2.4 bitcast_select_fusion
  307.6 13.2 %fusion.4 = f32[4,48,32,128]{3,2,1,0:T(8,128)} fusion(f32[4,48,32,128]{3,2,1,0:T(8,128)} %param.23, f32[4,48,1,128]{3,2,1,0:T(1,128)} %bitcast.16, f32[4,48,32,1]{3,2,1,0:T(8,128)} %copy.76, f32[4,48,32,1]{3,2,1,0:T(8,128)} %copy.74, f32[4,48,1,128]{3,2,1,0:T(1,128)S(1)} %bitcast.80, f32[4,48,31,128]{3,2,1,0:T(8,128)} %slice.222, ...), kind=kLoop, calls=%fused_computation.7 | loop fusion | flops 14155776 | bytes 16662528 | tf_op jit(solution)/shard_map/add | solution.py:294
  320.8 2.2 fusion.22
  323.1 2.2 fusion.21
  329.7 9.8 %all-to-all-start.1 = ((f32[2,128,2]{2,0,1:T(2,128)}), f32[2,128,2]{2,0,1:T(2,128)S(1)}, u32[]{:S(2)}, u32[]{:S(2)}) async-start(f32[2,128,2]{2,0,1:T(2,128)} %broadcast_select_fusion), calls=%async_computation.1 | async-start | bytes 262144 | tf_op jit(solution)/shard_map/all_to_all | solution.py:218
  339.7 9.8 %all-to-all-done.1 = f32[2,128,2]{2,0,1:T(2,128)S(1)} async-done(((f32[2,128,2]{2,0,1:T(2,128)}), f32[2,128,2]{2,0,1:T(2,128)S(1)}, u32[]{:S(2)}, u32[]{:S(2)}) %all-to-all-start.1) | async-done | bytes 2080 | tf_op jit(solution)/shard_map/all_to_all | solution.py:218
  (123 shorter events, 31.0 us)
Async XLA Ops:
  7.2 297.9 %all-gather.3.cloned.1.call-start = ((), (), s32[]{:S(2)}) async-start(), calls=%async_computation.2 | async-start | bytes 1671168 | tf_op jit(solution)/shard_map/all_gather | solution.py:276
  9.4 298.1 %collective-permute-start.15 = (f32[4,48,1,128]{3,1,0,2:T(8,128)S(1)}, f32[4,48,1,128]{3,1,0,2:T(8,128)}, u32[]{:S(2)}, u32[]{:S(2)}) collective-permute-start(f32[4,48,1,128]{3,1,0,2:T(8,128)S(1)} %bitcast.81), channel_id=1, source_target_pairs={{0,1},{1,2},{2,3},{3,4},{4,5},{5,6},{6,7},{8,9},{9,10},{10,11},{11... | collective-permute-start | bytes 294920 | tf_op jit(solution)/shard_map/ppermute | solution.py:29
  15.3 25.4 %collective-permute-start.1 = (f32[3,8,1,128]{3,2,1,0:T(1,128)S(1)}, f32[3,8,1,128]{3,2,1,0:T(1,128)S(1)}, u32[]{:S(2)}, u32[]{:S(2)}) collective-permute-start(f32[3,8,1,128]{3,2,1,0:T(1,128)S(1)} %get-tuple-element.53), channel_id=1, source_target_pairs={{8,0},{16,8},{24,16},{32,24},{40,32},{48,40},{56,48},{64,56},{72,6... | collective-permute-start | bytes 36872 | tf_op jit(solution)/shard_map/ppermute | solution.py:32
  16.3 24.4 %collective-permute-start = (f32[3,8,1,128]{3,2,1,0:T(1,128)S(1)}, f32[3,8,1,128]{3,2,1,0:T(1,128)S(1)}, u32[]{:S(2)}, u32[]{:S(2)}) collective-permute-start(f32[3,8,1,128]{3,2,1,0:T(1,128)S(1)} %get-tuple-element.73), channel_id=1, source_target_pairs={{0,8},{8,16},{16,24},{24,32},{32,40},{40,48},{48,56},{56,64},{64,7... | collective-permute-start | bytes 36872 | tf_op jit(solution)/shard_map/ppermute | solution.py:29
  28.1 266.9 %collective-permute-start.13 = (f32[4,48,32,1]{1,2,3,0:T(8,128)S(1)}, f32[4,48,32,1]{1,2,3,0:T(8,128)S(1)}, u32[]{:S(2)}, u32[]{:S(2)}) collective-permute-start(f32[4,48,32,1]{1,2,3,0:T(8,128)S(1)} %copy.94), channel_id=1, source_target_pairs={{0,8},{8,16},{16,24},{24,32},{32,40},{40,48},{48,56},{56,64},{64,7... | collective-permute-start | bytes 73736 | tf_op jit(solution)/shard_map/ppermute | solution.py:29
  30.4 268.3 %collective-permute-start.12 = (f32[4,48,32,1]{1,2,3,0:T(8,128)S(1)}, f32[4,48,32,1]{1,2,3,0:T(8,128)S(1)}, u32[]{:S(2)}, u32[]{:S(2)}) collective-permute-start(f32[4,48,32,1]{1,2,3,0:T(8,128)S(1)} %copy.93), channel_id=1, source_target_pairs={{8,0},{16,8},{24,16},{32,24},{40,32},{48,40},{56,48},{64,56},{72,6... | collective-permute-start | bytes 73736 | tf_op jit(solution)/shard_map/ppermute | solution.py:32
  31.8 14.5 %copy-start.10 = (s32[1,128,2]{1,2,0:T(2,128)S(1)}, s32[1,128,2]{1,2,0:T(2,128)}, u32[]{:S(2)}) copy-start(s32[1,128,2]{1,2,0:T(2,128)} %param.25) | copy-start | bytes 3076
  31.8 15.9 %copy-start.1 = (s32[4,8,16,128]{3,2,1,0:T(8,128)S(1)}, s32[4,8,16,128]{3,2,1,0:T(8,128)}, u32[]{:S(2)}) copy-start(s32[4,8,16,128]{3,2,1,0:T(8,128)} %param.20) | copy-start | bytes 786436
  31.8 15.9 %copy-start.3 = (f32[2,8,16,128]{3,2,1,0:T(8,128)S(1)}, f32[2,8,16,128]{3,2,1,0:T(8,128)}, u32[]{:S(2)}) copy-start(f32[2,8,16,128]{3,2,1,0:T(8,128)} %param.18) | copy-start | bytes 393220
  40.8 5.7 %collective-permute-start.3 = (f32[3,1,18,128]{3,2,1,0:T(8,128)S(1)}, f32[3,1,18,128]{3,2,1,0:T(8,128)S(1)}, u32[]{:S(2)}, u32[]{:S(2)}) collective-permute-start(f32[3,1,18,128]{3,2,1,0:T(8,128)S(1)} %get-tuple-element.68), channel_id=1, source_target_pairs={{1,0},{2,1},{3,2},{4,3},{5,4},{6,5},{7,6},{9,8},{10,9},{11,10},{12... | collective-permute-start | bytes 82952 | tf_op jit(solution)/shard_map/ppermute | solution.py:32
  42.1 5.5 %collective-permute-start.2 = (f32[3,1,18,128]{3,2,1,0:T(8,128)S(1)}, f32[3,1,18,128]{3,2,1,0:T(8,128)S(1)}, u32[]{:S(2)}, u32[]{:S(2)}) collective-permute-start(f32[3,1,18,128]{3,2,1,0:T(8,128)S(1)} %get-tuple-element.67), channel_id=1, source_target_pairs={{0,1},{1,2},{2,3},{3,4},{4,5},{5,6},{6,7},{8,9},{9,10},{10,11},{11... | collective-permute-start | bytes 82952 | tf_op jit(solution)/shard_map/ppermute | solution.py:29
  47.7 192.0 %copy-start.11 = (s32[1,128,2]{1,2,0:T(2,128)S(1)}, s32[1,128,2]{1,2,0:T(2,128)}, u32[]{:S(2)}) copy-start(s32[1,128,2]{1,2,0:T(2,128)} %param.22) | copy-start | bytes 3076
  100.0 4.7 %collective-permute-start.5 = (f32[3,8,1,128]{3,2,1,0:T(1,128)S(1)}, f32[3,8,1,128]{3,2,1,0:T(1,128)S(1)}, u32[]{:S(2)}, u32[]{:S(2)}) collective-permute-start(f32[3,8,1,128]{3,2,1,0:T(1,128)S(1)} %get-tuple-element.72), channel_id=1, source_target_pairs={{8,0},{16,8},{24,16},{32,24},{40,32},{48,40},{56,48},{64,56},{72,6... | collective-permute-start | bytes 36872 | tf_op jit(solution)/shard_map/ppermute | solution.py:32
  102.9 1.9 collective-permute-start.4
  104.8 5.5 %collective-permute-start.7 = (f32[3,1,18,128]{3,2,1,0:T(8,128)S(1)}, f32[3,1,18,128]{3,2,1,0:T(8,128)S(1)}, u32[]{:S(2)}, u32[]{:S(2)}) collective-permute-start(f32[3,1,18,128]{3,2,1,0:T(8,128)S(1)} %get-tuple-element.66), channel_id=1, source_target_pairs={{1,0},{2,1},{3,2},{4,3},{5,4},{6,5},{7,6},{9,8},{10,9},{11,10},{12... | collective-permute-start | bytes 82952 | tf_op jit(solution)/shard_map/ppermute | solution.py:32
  106.1 5.2 %collective-permute-start.6 = (f32[3,1,18,128]{3,2,1,0:T(8,128)S(1)}, f32[3,1,18,128]{3,2,1,0:T(8,128)S(1)}, u32[]{:S(2)}, u32[]{:S(2)}) collective-permute-start(f32[3,1,18,128]{3,2,1,0:T(8,128)S(1)} %get-tuple-element.65), channel_id=1, source_target_pairs={{0,1},{1,2},{2,3},{3,4},{4,5},{5,6},{6,7},{8,9},{9,10},{10,11},{11... | collective-permute-start | bytes 82952 | tf_op jit(solution)/shard_map/ppermute | solution.py:29
  164.4 4.7 %collective-permute-start.9 = (f32[3,8,1,128]{3,2,1,0:T(1,128)S(1)}, f32[3,8,1,128]{3,2,1,0:T(1,128)S(1)}, u32[]{:S(2)}, u32[]{:S(2)}) collective-permute-start(f32[3,8,1,128]{3,2,1,0:T(1,128)S(1)} %get-tuple-element.70), channel_id=1, source_target_pairs={{8,0},{16,8},{24,16},{32,24},{40,32},{48,40},{56,48},{64,56},{72,6... | collective-permute-start | bytes 36872 | tf_op jit(solution)/shard_map/ppermute | solution.py:32
  166.8 2.3 collective-permute-start.8
  169.2 5.3 %collective-permute-start.11 = (f32[3,1,18,128]{3,2,1,0:T(8,128)S(1)}, f32[3,1,18,128]{3,2,1,0:T(8,128)S(1)}, u32[]{:S(2)}, u32[]{:S(2)}) collective-permute-start(f32[3,1,18,128]{3,2,1,0:T(8,128)S(1)} %get-tuple-element.64), channel_id=1, source_target_pairs={{1,0},{2,1},{3,2},{4,3},{5,4},{6,5},{7,6},{9,8},{10,9},{11,10},{12... | collective-permute-start | bytes 82952 | tf_op jit(solution)/shard_map/ppermute | solution.py:32
  170.5 5.5 %collective-permute-start.10 = (f32[3,1,18,128]{3,2,1,0:T(8,128)S(1)}, f32[3,1,18,128]{3,2,1,0:T(8,128)S(1)}, u32[]{:S(2)}, u32[]{:S(2)}) collective-permute-start(f32[3,1,18,128]{3,2,1,0:T(8,128)S(1)} %get-tuple-element.63), channel_id=1, source_target_pairs={{0,1},{1,2},{2,3},{3,4},{4,5},{5,6},{6,7},{8,9},{9,10},{10,11},{11... | collective-permute-start | bytes 82952 | tf_op jit(solution)/shard_map/ppermute | solution.py:29
  174.5 130.6 %collective-permute-start.14 = (f32[4,48,1,128]{3,1,0,2:T(8,128)}, f32[4,48,1,128]{3,1,0,2:T(8,128)}, u32[]{:S(2)}, u32[]{:S(2)}) collective-permute-start(f32[4,48,1,128]{3,1,0,2:T(8,128)} %bitcast.32), channel_id=1, source_target_pairs={{1,0},{2,1},{3,2},{4,3},{5,4},{6,5},{7,6},{9,8},{10,9},{11,10},{12... | collective-permute-start | bytes 294920 | tf_op jit(solution)/shard_map/ppermute | solution.py:32
  240.8 61.5 %all-to-all-start = ((f32[2,128,2]{0,2,1:T(2,128)}), f32[2,128,2]{0,2,1:T(2,128)S(1)}, u32[]{:S(2)}, u32[]{:S(2)}) async-start(f32[2,128,2]{0,2,1:T(2,128)} %copy.82), calls=%async_computation | async-start | bytes 262144 | tf_op jit(solution)/shard_map/all_to_all | solution.py:214
  307.6 13.3 %copy-start.4 = (f32[4,48,32,128]{3,2,1,0:T(8,128)S(1)}, f32[4,48,32,128]{3,2,1,0:T(8,128)}, u32[]{:S(2)}) copy-start(f32[4,48,32,128]{3,2,1,0:T(8,128)} %param.23) | copy-start | bytes 9437188
  329.7 19.8 %all-to-all-start.1 = ((f32[2,128,2]{2,0,1:T(2,128)}), f32[2,128,2]{2,0,1:T(2,128)S(1)}, u32[]{:S(2)}, u32[]{:S(2)}) async-start(f32[2,128,2]{2,0,1:T(2,128)} %broadcast_select_fusion), calls=%async_computation.1 | async-start | bytes 262144 | tf_op jit(solution)/shard_map/all_to_all | solution.py:218
  (9 other events, 59.6 us)
Sparse Core Ops, SparseCore 0:
  14.5 50.3 all-gather.2
